TPU v7x, 256 devices: a whole 4x4x8 slice. The times are simulated.
256 devices in a mesh: req: 32 (over z_hi, y, core), tp: 8 (over x, z_lo).
Axes of the slice: x: 4, y: 4, z: 8 (z_hi: 4, z_lo: 2; z = z_hi * 2 + z_lo), core: 2. Of those that a mesh axis runs over, the one named last changes fastest.
Arguments:
- suffix: bfloat16 [256, 64, 2048], P('tp', 'req')
- prefix_store: bfloat16 [32, 2048, 2, 2048], P('req', None, None, 'tp')
- prefix_owner: int32 [2], replicated, may hold values from 0 to 31, as said below
- prefix_group: int32 [64], replicated, may hold values from 0 to 1
- request_perm: int32 [64], replicated, may hold values from 0 to 63, each once
- suffix_len: int32 [64], replicated, may hold values from 1 to 256, 8192 in all
- ln_gain_attn: float32 [2048], replicated, may hold values from 0.1 to 1.9
- w_qkv: bfloat16 [2048, 3, 2048], P(None, None, 'tp'), may hold values from -0.125 to 0.125
- w_out_attn: bfloat16 [2048, 2048], P('tp'), may hold values from -2.390625 to 2.390625
- ln_gain_mlp: float32 [2048], replicated, may hold values from 0.1 to 1.9
- w_in: bfloat16 [2048, 5120], P(None, 'tp'), may hold values from -0.125 to 0.125
- w_down: bfloat16 [5120, 2048], P('tp'), may hold values from -0.078125 to 0.078125
Outputs:
- layer_out: bfloat16 [256, 64, 2048], P('tp', 'req')
Inputs may be any that keep to these rules, and one draw needn't show every extreme that they name: `prefix_owner`: 2 different block indices. `request_perm`: each request exactly once.
All inputs are finite; a program needn't handle non-finite values.
Results may differ from a plain program's by a relative error of at most 0.015.
The roundings to bfloat16 on the way count: a program that leaves them out, or rounds other values in their place, can miss the bound.
Values may be sent and summed in bfloat16 or wider, within the bound.
A program may use at most 64 MiB of HBM per device.

v0:
```python
import jax
import jax.numpy as jnp
from jax import lax
from jax.sharding import PartitionSpec as P

HD = 128


def from_root(block, axis, source):
    block = jnp.where(lax.axis_index(axis) == source, block, jnp.zeros_like(block))
    return lax.psum(block, axis)


def layer_norm(values, gain):
    values = values.astype(jnp.float32)
    center = values - jnp.mean(values, -1, keepdims=True)
    spread = jnp.mean(center * center, -1, keepdims=True)
    return center * lax.rsqrt(spread + 1e-05) * gain


def fetch_prefixes(prefix_store, prefix_owner):
    caches = []
    for group in range(prefix_owner.shape[0]):
        caches.append(from_root(prefix_store[0], "req", prefix_owner[group]))
    return jnp.stack(caches)


def project_rows(suffix, gain, w_qkv):
    gathered = lax.all_gather(suffix, "tp", axis=0, tiled=True)
    normed = layer_norm(gathered, gain).astype(jnp.bfloat16)
    projected = jnp.einsum(
        "srd,dce->srce", normed, w_qkv, preferred_element_type=jnp.float32
    ).astype(jnp.bfloat16)
    return (projected, gathered)


def attend(projected, cached, lengths):
    slot_count, slots_dev, _, local_width = projected.shape
    heads = local_width // HD
    prefix_rows = cached.shape[1]
    scale = HD ** (-0.5)
    queries = projected[:, :, 0].reshape(slot_count, slots_dev, heads, HD)
    keys_own = projected[:, :, 1].reshape(slot_count, slots_dev, heads, HD)
    values_own = projected[:, :, 2].reshape(slot_count, slots_dev, heads, HD)
    keys_pre = cached[:, :, 0].reshape(slots_dev, prefix_rows, heads, HD)
    values_pre = cached[:, :, 1].reshape(slots_dev, prefix_rows, heads, HD)
    scores_pre = (
        jnp.einsum("srhd,rphd->rhsp", queries, keys_pre, preferred_element_type=jnp.float32) * scale
    )
    scores_own = (
        jnp.einsum("srhd,trhd->rhst", queries, keys_own, preferred_element_type=jnp.float32) * scale
    )
    places = jnp.arange(slot_count, dtype=jnp.int32)
    visible = (places[None, None, None, :] <= places[None, None, :, None]) & (
        places[None, None, None, :] < lengths[:, None, None, None]
    )
    scores_own = jnp.where(visible, scores_own, -jnp.inf)
    highest = jnp.maximum(
        jnp.max(scores_pre, -1, keepdims=True), jnp.max(scores_own, -1, keepdims=True)
    )
    raised_pre = jnp.exp(scores_pre - highest)
    raised_own = jnp.exp(scores_own - highest)
    total = jnp.sum(raised_pre, -1, keepdims=True) + jnp.sum(raised_own, -1, keepdims=True)
    weights_pre = (raised_pre / total).astype(jnp.bfloat16)
    weights_own = (raised_own / total).astype(jnp.bfloat16)
    context = jnp.einsum(
        "rhsp,rphd->srhd", weights_pre, values_pre, preferred_element_type=jnp.float32
    )
    context = context + jnp.einsum(
        "rhst,trhd->srhd", weights_own, values_own, preferred_element_type=jnp.float32
    )
    return context.reshape(slot_count, slots_dev, local_width).astype(jnp.bfloat16)


def on_device(
    suffix,
    prefix_store,
    prefix_owner,
    prefix_group,
    request_perm,
    suffix_len,
    ln_gain_attn,
    w_qkv,
    w_out_attn,
    ln_gain_mlp,
    w_in,
    w_down,
):
    part_rows, slots_dev, _ = suffix.shape
    slots = lax.axis_index("req") * slots_dev + jnp.arange(slots_dev, dtype=jnp.int32)
    requests = jnp.take(request_perm, slots)
    lengths = jnp.take(suffix_len, requests)
    groups = jnp.take(prefix_group, requests)
    stacked = fetch_prefixes(prefix_store, prefix_owner)
    projected, gathered = project_rows(suffix, ln_gain_attn, w_qkv)
    cached = jnp.take(stacked, groups, axis=0)
    context = attend(projected, cached, lengths)
    first_row = lax.axis_index("tp") * part_rows
    block = context
    attention = lax.psum_scatter(
        jnp.einsum("srk,kd->srd", block, w_out_attn, preferred_element_type=jnp.float32).astype(
            jnp.bfloat16
        ),
        "tp",
        scatter_dimension=0,
        tiled=True,
    ).astype(jnp.float32)
    hidden = (suffix.astype(jnp.float32) + attention).astype(jnp.bfloat16)
    normed = layer_norm(hidden, ln_gain_mlp).astype(jnp.bfloat16)
    product = jnp.einsum(
        "srd,df->srf",
        lax.all_gather(normed, "tp", axis=0, tiled=True),
        w_in,
        preferred_element_type=jnp.float32,
    )
    inner = jax.nn.gelu(product, approximate=False).astype(jnp.bfloat16)
    block = inner
    down = lax.psum_scatter(
        jnp.einsum("srf,fd->srd", block, w_down, preferred_element_type=jnp.float32).astype(
            jnp.bfloat16
        ),
        "tp",
        scatter_dimension=0,
        tiled=True,
    ).astype(jnp.float32)
    places = first_row + jnp.arange(part_rows, dtype=jnp.int32)
    valid = places[:, None] < lengths[None, :]
    return jnp.where(valid[:, :, None], hidden.astype(jnp.float32) + down, 0.0).astype(jnp.bfloat16)


def solution(mesh):
    placed = (
        P("tp", "req", None),
        P("req", None, None, "tp"),
        P(),
        P(),
        P(),
        P(),
        P(),
        P(None, None, "tp"),
        P("tp", None),
        P(),
        P(None, "tp"),
        P("tp", None),
    )
    return jax.shard_map(
        on_device, mesh=mesh, in_specs=placed, out_specs=P("tp", "req", None), check_vma=False
    )
```

profile of v0, /device:TPU:1, one launch (start us, length us, event | category | flops | bytes accessed | tf_op | source)
XLA Modules:
  0.0 555.5 jit_solution(3519037379020641564)
XLA Ops:
  8.1 1.4 fusion.112
  10.8 4.0 broadcast_select_fusion
  17.7 54.1 %all-gather.3.cloned.1.call-done = bf16[256,2,2048]{2,1,0:T(2,128)(2,1)} async-done(((bf16[32,2,2048]{2,1,0:T(2,128)(2,1)}), bf16[256,2,2048]{2,1,0:T(2,128)(2,1)}) %all-gather.3.cloned.1.call-update) | async-done | bytes 2097168 | tf_op jit(solution)/shard_map/all_gather | solution.py:29
  71.8 3.4 convert_reduce_fusion
  75.3 2.9 fusion.3
  78.2 3.3 fusion.12
  81.5 1.9 fusion.14
  84.5 254.9 %all-reduce.3.cloned.1.call-done = (bf16[1,2048,2,256]{3,1,2,0:T(8,128)(2,1)}, bf16[1,2048,2,256]{3,1,2,0:T(8,128)(2,1)}) async-done(((bf16[1,2048,2,256]{3,1,2,0:T(8,128)(2,1)}, bf16[1,2048,2,256]{3,1,2,0:T(8,128)(2,1)}), (bf16[1,2048,2,256]{3,1,2,0:T(8,128)(2,1)}, bf16[1,2048,2,256]{3,1,2,0:T(8,128)(2,1)})) %all-reduce.3.cloned.1.call-update) | async-done | bytes 4194320 | tf_op jit(solution)/shard_map/psum | solution.py:11
  339.5 1.9 constant_dynamic-update-slice_fusion.1
  341.8 2.2 fusion.110
  344.0 2.3 gather_fusion.1
  346.3 3.6 gather_fusion
  349.9 2.8 maximum_select_fusion
  352.7 1.6 fusion.109
  354.3 2.5 copy.50
  356.8 2.9 copy.53
  361.2 1.6 fusion
  363.0 2.8 fusion.6
  367.1 2.1 convolution_convert_fusion
  369.2 54.1 %reduce-scatter.3.cloned.1.call-done = bf16[32,2,2048]{2,0,1:T(8,128)(2,1)} async-done(((bf16[256,2,2048]{2,0,1:T(8,128)(2,1)}), bf16[32,2,2048]{2,0,1:T(8,128)(2,1)}) %reduce-scatter.3.cloned.1.call-update) | async-done | bytes 262160 | tf_op jit(solution)/shard_map/reduce_scatter | solution.py:100
  425.7 54.0 %all-gather.5.cloned.1.call-done = bf16[256,2,2048]{2,0,1:T(8,128)(2,1)} async-done(((bf16[32,2,2048]{2,0,1:T(8,128)(2,1)}), bf16[256,2,2048]{2,0,1:T(8,128)(2,1)}) %all-gather.5.cloned.1.call-update) | async-done | bytes 2097168 | tf_op jit(solution)/shard_map/all_gather | solution.py:112
  479.7 4.4 fusion.74
  484.1 7.7 %convolution_convert_fusion.1 = bf16[256,2,2048]{2,0,1:T(8,128)(2,1)} fusion(bf16[640,2048]{1,0:T(8,128)(2,1)} %param.25, f32[256,2,640]{2,0,1:T(8,128)S(1)} %get-tuple-element.29, u8[256,640]{1,0:T(8,128)(4,1)S(1)} %get-tuple-element.7, u8[256,640]{1,0:T(8,128)(4,1)S(1)} %get-tuple-element.6), kind=kOutput, calls=%fused_computation.21 | convolution fusion | flops 1366163456 | bytes 6356992 | tf_op jit(solution)/shard_map/srf,fd->srd/dot_general | solution.py:119
  492.0 54.4 %reduce-scatter.5.cloned.1.call-done = bf16[32,2,2048]{2,0,1:T(8,128)(2,1)} async-done(((bf16[256,2,2048]{2,0,1:T(8,128)(2,1)}), bf16[32,2,2048]{2,0,1:T(8,128)(2,1)}) %reduce-scatter.5.cloned.1.call-update) | async-done | bytes 262160 | tf_op jit(solution)/shard_map/reduce_scatter | solution.py:118
  (68 shorter events, 12.5 us)
Async XLA Ops:
  7.4 74.2 %copy-start = (bf16[2048,3,256]{2,0,1:T(8,128)(2,1)S(1)}, bf16[2048,3,256]{2,0,1:T(8,128)(2,1)}, u32[]{:S(2)}) copy-start(bf16[2048,3,256]{2,0,1:T(8,128)(2,1)} %param.21) | copy-start | bytes 9437188
  7.4 64.5 %all-gather.3.cloned.1.call-start = ((), (), s32[]{:S(2)}) async-start(), calls=%async_computation.2 | async-start | bytes 2359296 | tf_op jit(solution)/shard_map/all_gather | solution.py:29
  8.1 331.4 %all-reduce.3.cloned.1.call-start = ((), (), s32[]{:S(2)}) async-start(), calls=%async_computation.6 | async-start | bytes 8388608 | tf_op jit(solution)/shard_map/psum | solution.py:11
  14.8 0.7 copy-start.2
  14.8 1.3 copy-start.3
  14.8 2.0 copy-start.4
  14.8 408.5 %reduce-scatter.3.cloned.1.call-start = ((), (), s32[]{:S(2)}) async-start(), calls=%async_computation.3 | async-start | bytes 2359296 | tf_op jit(solution)/shard_map/reduce_scatter | solution.py:100
  17.7 60.5 %copy-start.11 = (f32[2048]{0:T(1024)S(1)}, f32[2048]{0:T(1024)}, u32[]{:S(2)}) copy-start(f32[2048]{0:T(1024)} %param.20) | copy-start | bytes 24580
  71.8 3.5 copy-start.5
  339.5 2.2 copy-start.6
  361.2 1.8 copy-start.7
  363.0 2.8 copy-start.10
  365.9 1.2 copy-start.8
  367.1 56.3 %copy-start.9 = (bf16[32,2,2048]{2,1,0:T(2,128)(2,1)S(1)}, bf16[32,2,2048]{2,1,0:T(2,128)(2,1)}, u32[]{:S(2)}) copy-start(bf16[32,2,2048]{2,1,0:T(2,128)(2,1)} %param.14) | copy-start | bytes 786436
  369.2 55.6 %copy-start.12 = (f32[2048]{0:T(1024)S(1)}, f32[2048]{0:T(1024)}, u32[]{:S(2)}) copy-start(f32[2048]{0:T(1024)} %param.23) | copy-start | bytes 24580
  369.2 110.5 %all-gather.5.cloned.1.call-start = ((), (), s32[]{:S(2)}) async-start(), calls=%async_computation.4 | async-start | bytes 2359296 | tf_op jit(solution)/shard_map/all_gather | solution.py:112
  425.6 120.7 %reduce-scatter.5.cloned.1.call-start = ((), (), s32[]{:S(2)}) async-start(), calls=%async_computation.5 | async-start | bytes 2359296 | tf_op jit(solution)/shard_map/reduce_scatter | solution.py:118
  484.1 64.3 %copy-start.1 = (bf16[2048,3,256]{2,0,1:T(8,128)(2,1)S(1)}, bf16[2048,3,256]{2,0,1:T(8,128)(2,1)}, u32[]{:S(2)}) copy-start(bf16[2048,3,256]{2,0,1:T(8,128)(2,1)} %param.21) | copy-start | bytes 9437188
Sparse Core Ops, SparseCore 0:
  10.0 61.8 all-gather.2
  369.3 53.9 reduce-scatter.2
  425.7 53.9 all-gather.4
  492.0 54.2 reduce-scatter.4
Sparse Core Ops, SparseCore 1:
  14.9 324.5 all-reduce.2
where the time goes:
time: 556 us; the launch traced here: 555 us
  waiting for transfers between devices  472 us (85%)
  local copies, waits for them, and re-layouts  23.9 us (4%)
  other arithmetic  21.9 us (4%)
  matrix products  21 us (4%)
  between operations  16.1 us (3%)
    psum x1, waiting for transfers between devices, from_root(): return lax.psum(block, axis)  255 us
    reduce_scatter x1, waiting for transfers between devices, on_device(): lax.psum_scatter(jnp.einsum('srf,fd->srd', block, w_down, preferred_eleme...  54.4 us
    reduce_scatter x1, waiting for transfers between devices, on_device(): lax.psum_scatter(jnp.einsum('srk,kd->srd', block, w_out_attn, preferred_e...  54.1 us
    all_gather x1, waiting for transfers between devices, project_rows(): gathered = lax.all_gather(suffix, 'tp', axis=0, tiled=True)  54.1 us
    all_gather x1, waiting for transfers between devices, on_device(): lax.all_gather(normed, 'tp', axis=0, tiled=True)  54 us
  transfers between devices with their start and end apart: 5, of which 5 were waited for; matrix products, arithmetic and copies ran while one was open for 4% of the time, Pallas kernels for 0%

commit v1 on v0

--- a/solution.py
+++ b/solution.py
@@ -4,6 +4,13 @@
 from jax.sharding import PartitionSpec as P
 
 HD = 128
+
+
+def exchange_gather(x, mesh_axis, d):
+    count = lax.axis_size(mesh_axis)
+    pieces = jnp.stack([x for _ in range(count)])
+    pieces = lax.all_to_all(pieces, mesh_axis, split_axis=0, concat_axis=0)
+    return jnp.concatenate(pieces, axis=d)
 
 
 def from_root(block, axis, source):
@@ -108,10 +115,7 @@
     hidden = (suffix.astype(jnp.float32) + attention).astype(jnp.bfloat16)
     normed = layer_norm(hidden, ln_gain_mlp).astype(jnp.bfloat16)
     product = jnp.einsum(
-        "srd,df->srf",
-        lax.all_gather(normed, "tp", axis=0, tiled=True),
-        w_in,
-        preferred_element_type=jnp.float32,
+        "srd,df->srf", exchange_gather(normed, "tp", 0), w_in, preferred_element_type=jnp.float32
     )
     inner = jax.nn.gelu(product, approximate=False).astype(jnp.bfloat16)
     block = inner

time: 556 us -> 529 us (0.951)
  waiting for transfers between devices: 472 us -> 420 us
  blocking collectives: 0 us -> 29.2 us
    all_gather x1 -> x0, waiting for transfers between devices: 54 us -> none  [on_device(): lax.all_gather(normed, 'tp', axis=0, tiled=True)]
    all_to_all x0 -> x1, blocking collectives: none -> 29.2 us  [exchange_gather(): pieces = lax.all_to_all(pieces, mesh_axis, split_axis=0, concat_axis=0)]
  transfers between devices with their start and end apart: 5 -> 4, of which waited for: 5 -> 4; matrix products, arithmetic and copies ran while one was open for 4% -> 4% of each run, Pallas kernels for 0% -> 0%
where the time goes in v1:
time: 529 us
  waiting for transfers between devices  420 us (79%)
  blocking collectives  29.2 us (6%)
  local copies, waits for them, and re-layouts  26 us (5%)
  other arithmetic  21.3 us (4%)
  matrix products  16.5 us (3%)
  between operations  16.1 us (3%)
    psum x1, waiting for transfers between devices, from_root(): return lax.psum(block, axis)  255 us
    reduce_scatter x1, waiting for transfers between devices, on_device(): lax.psum_scatter(jnp.einsum('srf,fd->srd', block, w_down, preferred_eleme...  55.5 us
    reduce_scatter x1, waiting for transfers between devices, on_device(): lax.psum_scatter(jnp.einsum('srk,kd->srd', block, w_out_attn, preferred_e...  54.4 us
    all_gather x1, waiting for transfers between devices, project_rows(): gathered = lax.all_gather(suffix, 'tp', axis=0, tiled=True)  54.1 us
    all_to_all x1, blocking collectives, exchange_gather(): pieces = lax.all_to_all(pieces, mesh_axis, split_axis=0, concat_axis=0)  29.2 us
  transfers between devices with their start and end apart: 4, of which 4 were waited for; matrix products, arithmetic and copies ran while one was open for 4% of the time, Pallas kernels for 0%

profile of v1, /device:TPU:1, one launch (start us, length us, event | category | flops | bytes accessed | tf_op | source)
XLA Modules:
  0.0 528.8 jit_solution(14196647458555126264)
XLA Ops:
  10.8 4.0 broadcast_select_fusion
  17.7 54.1 %all-gather.2.cloned.1.call-done = bf16[256,2,2048]{2,1,0:T(2,128)(2,1)} async-done(((bf16[32,2,2048]{2,1,0:T(2,128)(2,1)}), bf16[256,2,2048]{2,1,0:T(2,128)(2,1)}) %all-gather.2.cloned.1.call-update) | async-done | bytes 2097168 | tf_op jit(solution)/shard_map/all_gather | solution.py:36
  71.8 3.4 convert_reduce_fusion
  75.3 2.9 fusion.3
  78.2 3.3 fusion.12
  81.5 1.9 fusion.14
  84.5 254.8 %all-reduce.3.cloned.1.call-done = (bf16[1,2048,2,256]{3,1,2,0:T(8,128)(2,1)}, bf16[1,2048,2,256]{3,1,2,0:T(8,128)(2,1)}) async-done(((bf16[1,2048,2,256]{3,1,2,0:T(8,128)(2,1)}, bf16[1,2048,2,256]{3,1,2,0:T(8,128)(2,1)}), (bf16[1,2048,2,256]{3,1,2,0:T(8,128)(2,1)}, bf16[1,2048,2,256]{3,1,2,0:T(8,128)(2,1)})) %all-reduce.3.cloned.1.call-update) | async-done | bytes 4194320 | tf_op jit(solution)/shard_map/psum | solution.py:18
  339.3 1.9 constant_dynamic-update-slice_fusion.1
  341.7 2.2 fusion.110
  343.9 2.3 gather_fusion.1
  346.2 3.6 gather_fusion
  349.7 2.8 maximum_select_fusion
  352.6 1.6 fusion.109
  354.2 2.5 copy.50
  356.7 2.9 copy.53
  361.0 1.6 fusion
  362.9 2.8 fusion.6
  366.9 2.1 convolution_convert_fusion
  369.1 54.4 %reduce-scatter.3.cloned.1.call-done = bf16[32,2,2048]{2,0,1:T(8,128)(2,1)} async-done(((bf16[256,2,2048]{2,0,1:T(8,128)(2,1)}), bf16[32,2,2048]{2,0,1:T(8,128)(2,1)}) %reduce-scatter.3.cloned.1.call-update) | async-done | bytes 262160 | tf_op jit(solution)/shard_map/reduce_scatter | solution.py:107
  425.3 29.2 %all_to_all.5 = bf16[8,32,2,2048]{3,1,2,0:T(8,128)(2,1)S(1)} all-to-all(bf16[8,32,2,2048]{3,1,2,0:T(8,128)(2,1)S(1)} %stack.11), channel_id=1, replica_groups=mesh['req'=32,'tp'=8] {'tp'}, dimensions={0} | all-to-all | bytes 4194304 | tf_op jit(solution)/shard_map/all_to_all | solution.py:12
  454.7 1.6 copy-done.13
  456.3 2.0 fusion.74
  458.3 5.7 %convolution_convert_fusion.1 = bf16[256,2,2048]{2,0,1:T(8,128)(2,1)} fusion(bf16[640,2048]{1,0:T(8,128)(2,1)S(1)} %copy-done.14, f32[256,2,640]{2,0,1:T(8,128)S(1)} %get-tuple-element.29, u8[256,640]{1,0:T(8,128)(4,1)S(1)} %get-tuple-element.7, u8[256,640]{1,0:T(8,128)(4,1)S(1)} %get-tuple-element.6), kind=kOutput, calls=%fused_computation.21 | convolution fusion | flops 1366163456 | bytes 6356992 | tf_op jit(solution)/shard_map/srf,fd->srd/dot_general | solution.py:123
  464.1 55.5 %reduce-scatter.5.cloned.1.call-done = bf16[32,2,2048]{2,0,1:T(8,128)(2,1)} async-done(((bf16[256,2,2048]{2,0,1:T(8,128)(2,1)}), bf16[32,2,2048]{2,0,1:T(8,128)(2,1)}) %reduce-scatter.5.cloned.1.call-update) | async-done | bytes 262160 | tf_op jit(solution)/shard_map/reduce_scatter | solution.py:122
  (72 shorter events, 13.6 us)
Async XLA Ops:
  7.4 74.2 %copy-start = (bf16[2048,3,256]{2,0,1:T(8,128)(2,1)S(1)}, bf16[2048,3,256]{2,0,1:T(8,128)(2,1)}, u32[]{:S(2)}) copy-start(bf16[2048,3,256]{2,0,1:T(8,128)(2,1)} %param.21) | copy-start | bytes 9437188
  7.4 64.5 %all-gather.2.cloned.1.call-start = ((), (), s32[]{:S(2)}) async-start(), calls=%async_computation.3 | async-start | bytes 2359296 | tf_op jit(solution)/shard_map/all_gather | solution.py:36
  8.1 331.2 %all-reduce.3.cloned.1.call-start = ((), (), s32[]{:S(2)}) async-start(), calls=%async_computation.6 | async-start | bytes 8388608 | tf_op jit(solution)/shard_map/psum | solution.py:18
  14.8 0.7 copy-start.2
  14.8 1.3 copy-start.3
  14.8 2.0 copy-start.4
  14.8 408.6 %reduce-scatter.3.cloned.1.call-start = ((), (), s32[]{:S(2)}) async-start(), calls=%async_computation.4 | async-start | bytes 2359296 | tf_op jit(solution)/shard_map/reduce_scatter | solution.py:107
  17.7 60.5 %copy-start.11 = (f32[2048]{0:T(1024)S(1)}, f32[2048]{0:T(1024)}, u32[]{:S(2)}) copy-start(f32[2048]{0:T(1024)} %param.20) | copy-start | bytes 24580
  71.8 3.5 copy-start.5
  339.3 2.2 copy-start.6
  361.0 1.8 copy-start.7
  362.9 2.8 copy-start.10
  365.7 1.2 copy-start.8
  366.9 56.5 %copy-start.9 = (bf16[32,2,2048]{2,1,0:T(2,128)(2,1)S(1)}, bf16[32,2,2048]{2,1,0:T(2,128)(2,1)}, u32[]{:S(2)}) copy-start(bf16[32,2,2048]{2,1,0:T(2,128)(2,1)} %param.14) | copy-start | bytes 786436
  369.0 55.8 %copy-start.12 = (f32[2048]{0:T(1024)S(1)}, f32[2048]{0:T(1024)}, u32[]{:S(2)}) copy-start(f32[2048]{0:T(1024)} %param.23) | copy-start | bytes 24580
  369.1 150.6 %reduce-scatter.5.cloned.1.call-start = ((), (), s32[]{:S(2)}) async-start(), calls=%async_computation.5 | async-start | bytes 2359296 | tf_op jit(solution)/shard_map/reduce_scatter | solution.py:122
  454.5 1.7 copy-start.13
  456.3 2.0 copy-start.14
  458.3 63.3 %copy-start.1 = (bf16[2048,3,256]{2,0,1:T(8,128)(2,1)S(1)}, bf16[2048,3,256]{2,0,1:T(8,128)(2,1)}, u32[]{:S(2)}) copy-start(bf16[2048,3,256]{2,0,1:T(8,128)(2,1)} %param.21) | copy-start | bytes 9437188
Sparse Core Ops, SparseCore 0:
  10.0 61.8 all-gather.1
  369.2 54.2 reduce-scatter.2
  464.1 55.4 reduce-scatter.4
Sparse Core Ops, SparseCore 1:
  14.9 324.3 all-reduce.2
